TPU v7x, 32 devices: a whole 2x2x4 slice. The times are simulated.
32 devices in a mesh: cube: 2 (over core), row: 4 (over y, x), col: 4 (over z).
Axes of the slice: x: 2, y: 2, z: 4, core: 2. Of those that a mesh axis runs over, the one named last changes fastest.
Arguments:
- child_update: float32 [2, 8192, 8192], P('cube', 'row', 'col'), may hold values from -8 to 80, as said below
- child_panel: bfloat16 [2, 8192, 2048], P('cube', 'row'), may hold values from -8 to 8
- parent_front: bfloat16 [16384, 16384], P('row', ('cube', 'col')), may hold values from -8 to 520, as said below
- block_map: int32 [2, 64], replicated, may hold values from 0 to 127, as said below
Outputs:
- schur: float32 [16384, 16384], P('row', ('cube', 'col'))
- panel: float32 [16384, 512], P('row')
Inputs may be any that keep to these rules, and one draw needn't show every extreme that they name: child_update[k] is symmetric for every child. parent_front is symmetric, and the leading 512 x 512 block of front is positive definite. `block_map`: for each child the 64 entries are distinct. Split a child's entries into aligned groups of 16 entries. In every group, for each r from 0 to 3, exactly 4 entries e have e // 32 equal to r. In every group, at most 2 entries share one value of e // 16, and every group has a value shared by 2 entries.
All inputs are finite; a program needn't handle non-finite values.
Results may differ from a plain program's by a relative error of at most 0.00044.
Values may be sent and summed in bfloat16 or wider, within the bound.
A program may use at most 320 MiB of HBM per device.

v0:
```python
import jax
import jax.numpy as jnp
from jax import lax
from jax.sharding import PartitionSpec as P

BLK = 128
PANEL = 512


def broadcast(block, axis, holder):
    block = jnp.where(lax.axis_index(axis) == holder, block, jnp.zeros_like(block))
    return lax.psum(block, axis)


def group_ranks(labels):
    count_all = labels.shape[-1]
    position = jnp.arange(count_all)
    before = position[:, None] > position[None, :]
    same_label = labels[..., :, None] == labels[..., None, :]
    return jnp.sum(jnp.logical_and(same_label, before), axis=-1)


def slot_tables(block_map, grid_rows, grid_cols, row_cap, col_cap, range_rows, range_cols):
    children = block_map.shape[0]
    grouped = block_map.reshape(children, grid_rows, -1)
    group_blocks = grouped.shape[2]
    row_dest = grouped // range_rows
    col_dest = grouped // range_cols
    row_slot = row_dest * row_cap + group_ranks(row_dest)
    col_slot = col_dest * col_cap + group_ranks(col_dest)
    members = jnp.arange(group_blocks, dtype=jnp.int32)
    row_hits = (row_slot[..., :, None] == members).astype(jnp.int32)
    send_rows = jnp.sum(row_hits * members[:, None], axis=2)
    row_local = jnp.sum(row_hits * (grouped % range_rows)[..., None], axis=2)
    col_slots = jnp.arange(grid_cols * col_cap, dtype=jnp.int32)
    col_hits = (col_slot[..., :, None] == col_slots).astype(jnp.int32)
    filled = jnp.sum(col_hits, axis=2) > 0
    send_cols = jnp.where(filled, jnp.sum(col_hits * members[:, None], axis=2), group_blocks)
    col_local = jnp.where(filled, jnp.sum(col_hits * (grouped % range_cols)[..., None], axis=2), -1)
    return (send_rows, row_local, send_cols, col_local)


def solve_rows(factor, raw_rows):
    result_rows = jax.scipy.linalg.solve_triangular(factor, raw_rows.T, lower=True).T
    return result_rows


def body(child_update, child_panel, parent_front, block_map):
    grid_rows = lax.axis_size("row")
    cube_count = lax.axis_size("cube")
    col_count = lax.axis_size("col")
    grid_cols = cube_count * col_count
    child_index = lax.axis_index("cube")
    row_index = lax.axis_index("row")
    col_index = lax.axis_index("col")
    range_index = lax.axis_index(("cube", "col"))
    group_blocks = child_update.shape[1] // BLK
    row_cap = group_blocks // grid_rows
    col_cap = max(1, group_blocks // grid_cols)
    front_rows, front_cols = parent_front.shape
    range_rows = front_rows // BLK
    range_cols = front_cols // BLK
    tiles_total = range_rows * range_cols
    own_panel = child_panel[0]
    column_panel = broadcast(own_panel, "row", col_index)
    contribution = child_update[0] - lax.dot_general(
        own_panel, column_panel, (((1,), (1,)), ((), ())), preferred_element_type=jnp.float32
    )
    send_rows, row_local, send_cols, col_local = slot_tables(
        block_map, grid_rows, grid_cols, row_cap, col_cap, range_rows, range_cols
    )
    my_rows = send_rows[child_index, row_index]
    my_cols = send_cols[child_index, col_index]
    blocks = contribution.reshape(group_blocks, BLK, group_blocks, BLK)
    by_row = jnp.take(blocks, my_rows, axis=0)
    incoming_rows = lax.dynamic_slice_in_dim(row_local, row_index * row_cap, row_cap, 2)
    incoming_cols = lax.dynamic_slice_in_dim(col_local, range_index * col_cap, col_cap, 2)
    packed = jnp.take(by_row, my_cols, axis=2, mode="fill", fill_value=0.0)
    packed = packed.reshape(grid_rows, row_cap, BLK, cube_count, col_count, col_cap, BLK)
    packed = packed.transpose(3, 0, 4, 1, 2, 5, 6).reshape(
        cube_count * grid_rows * col_count, row_cap * BLK, col_cap * BLK
    )
    arrived = lax.all_to_all(
        packed, ("cube", "row", "col"), split_axis=0, concat_axis=0, tiled=True
    )
    arrived = arrived.reshape(
        cube_count, grid_rows, col_count, row_cap, BLK, col_cap, BLK
    ).transpose(0, 1, 2, 3, 5, 4, 6)
    target_rows = incoming_rows[:, :, None, :, None]
    target_cols = incoming_cols[:, None, :, None, :]
    targets = jnp.where(target_cols >= 0, target_rows * range_cols + target_cols, tiles_total)
    pieces = arrived.reshape(-1, BLK, BLK)
    summed = jax.ops.segment_sum(pieces, targets.reshape(-1), num_segments=tiles_total)
    assembled = (
        summed.reshape(range_rows, range_cols, BLK, BLK)
        .transpose(0, 2, 1, 3)
        .reshape(front_rows, front_cols)
    )
    front_tile = parent_front.astype(jnp.float32) + assembled
    pivot_block = broadcast(front_tile[:PANEL, :PANEL], "row", 0)
    local_factor = jnp.linalg.cholesky(pivot_block)
    global_rows = row_index * front_rows + jnp.arange(front_rows)
    pivot_rows = global_rows[:, None] < PANEL

    def finish_rows(factor, solved):
        padded_pivot = jnp.concatenate(
            [factor, jnp.zeros((front_rows - PANEL, PANEL), jnp.float32)], axis=0
        )
        return jnp.where(pivot_rows, padded_pivot, solved)

    owner_rows = lax.cond(
        range_index == 0,
        lambda: finish_rows(local_factor, solve_rows(local_factor, front_tile[:, :PANEL])),
        lambda: jnp.zeros((front_rows, PANEL), jnp.float32),
    )
    panel_rows = broadcast(owner_rows, ("cube", "col"), 0)
    panel_low = panel_rows.astype(jnp.bfloat16)
    first_col = range_index * front_cols
    crossed = broadcast(panel_low, "row", first_col // front_rows)
    column_low = lax.dynamic_slice_in_dim(crossed, first_col % front_rows, front_cols, 0)
    update = front_tile - lax.dot_general(
        panel_low, column_low, (((1,), (1,)), ((), ())), preferred_element_type=jnp.float32
    )
    global_cols = first_col + jnp.arange(front_cols)
    keep_mask = (global_rows[:, None] >= PANEL) & (global_cols[None, :] >= PANEL)
    schur_tile = jnp.where(keep_mask, update, jnp.zeros_like(update))
    return (schur_tile, panel_rows)


def solution(mesh):
    placed = (P("cube", "row", "col"), P("cube", "row", None), P("row", ("cube", "col")), P())
    return jax.shard_map(
        body,
        mesh=mesh,
        in_specs=placed,
        out_specs=(P("row", ("cube", "col")), P("row", None)),
        check_vma=False,
    )
```

profile of v0, /device:TPU:0, one launch (start us, length us, event | category | flops | bytes accessed | tf_op | source)
XLA Modules:
  0.0 1508.2 jit_solution(11700483400209119964)
XLA Ops:
  7.2 7.3 bitcast_select_fusion
  15.3 17.8 %copy.60 = f32[1,2048,2048]{1,2,0:T(8,128)} copy(f32[1,2048,2048]{2,1,0:T(8,128)} %param.6) | data formatting | bytes 33554432 | tf_op args[0]
  35.2 154.3 %all-reduce.7.cloned.1.call-done = bf16[2048,2048]{1,0:T(8,128)(2,1)} async-done(((bf16[2048,2048]{1,0:T(8,128)(2,1)}), bf16[2048,2048]{1,0:T(8,128)(2,1)}) %all-reduce.7.cloned.1.call-update) | async-done | bytes 8388624 | tf_op jit(solution)/shard_map/psum | solution.py:12
  189.5 26.3 %fusion.24 = f32[256,8,16,128]{3,1,2,0:T(8,128)} fusion(f32[1,2048,2048]{1,2,0:T(8,128)} %copy.60, bf16[2048,2048]{1,0:T(8,128)(2,1)} %all-reduce.7.cloned.1.call-done, bf16[1,2048,2048]{2,1,0:T(8,128)(2,1)} %param.7), kind=kOutput, calls=%fused_computation.51 | convolution fusion | flops 17184063488 | bytes 50331648 | tf_op jit(solution)/shard_map/dot_general | solution.py:66
  215.8 14.2 copy.81
  229.9 21.5 %copy.61 = f32[16,128,16,128]{3,2,1,0:T(8,128)} copy(f32[16,128,16,128]{1,0,3,2:T(8,128)} %bitcast.101) | data formatting | bytes 33554432 | tf_op jit(solution)/shard_map/reshape | solution.py:74
  251.4 14.3 gather_fusion
  265.7 6.9 broadcast_select_fusion
  272.6 8.0 copy.62
  280.6 14.3 gather_fusion.1
  294.9 29.3 %fusion.25 = f32[2,4,4,4,128,2,128]{6,5,4,3,2,1,0:T(2,128)} fusion(f32[4,4,128,2,4,2,128]{6,2,1,0,5,4,3:T(8,128)} %bitcast.99, pred[2,4,2]{2,1,0:T(4,128)(4,1)S(1)} %compare_and_fusion), kind=kLoop, calls=%fused_computation.53 | loop fusion | flops 4194304 | bytes 33554448 | tf_op jit(solution)/shard_map/transpose | solution.py:80
  324.1 21.6 %reshape.390 = f32[32,512,256]{2,1,0:T(8,128)} reshape(f32[2,4,4,4,128,2,128]{6,5,4,3,2,1,0:T(2,128)} %fusion.25) | data formatting | bytes 33554432 | tf_op jit(solution)/shard_map/reshape | solution.py:80
  345.7 5.3 all-to-all-start
  351.5 20.9 %copy.59 = bf16[4096,2048]{0,1:T(8,128)(2,1)} copy(bf16[4096,2048]{1,0:T(8,128)(2,1)} %param.8) | data formatting | bytes 33554432 | tf_op args[2]
  372.4 336.7 %all-to-all-done = f32[32,512,256]{2,1,0:T(8,128)} async-done(((f32[32,512,256]{2,1,0:T(8,128)}), f32[32,512,256]{2,1,0:T(8,128)}, u32[]{:S(2)}, u32[]{:S(2)}) %all-to-all-start) | async-done | bytes 16777248 | tf_op jit(solution)/shard_map/all_to_all | solution.py:83
  709.1 20.8 %reshape.391 = f32[2,4,4,4,128,2,128]{6,5,4,3,2,1,0:T(2,128)} reshape(f32[32,512,256]{2,1,0:T(8,128)} %all-to-all-done) | data formatting | bytes 33554432 | tf_op jit(solution)/shard_map/reshape | solution.py:86
  729.9 12.7 copy.64
  742.6 11.5 broadcast_in_dim.87
  754.0 51.6 %scatter_fusion = f32[512,128,128]{2,1,0:T(8,128)} fusion(f32[512,128,128]{2,1,0:T(8,128)} %broadcast_in_dim.87, s32[256]{0:T(256)S(1)} %reshape.432, f32[256,128,128]{2,1,0:T(8,128)} %bitcast.100), kind=kCustom, calls=%fused_computation.2 | custom fusion | flops 4194304 | bytes 50332672 | tf_op jit(solution)/shard_map/scatter-add | solution.py:93
  805.6 34.6 %copy.65 = f32[32,128,16,128]{1,0,3,2:T(8,128)} copy(f32[32,128,16,128]{3,1,2,0:T(8,128)} %bitcast.97) | data formatting | bytes 67108864 | tf_op jit(solution)/shard_map/transpose | solution.py:96
  840.2 37.0 %bitcast_add_fusion = f32[4096,2048]{0,1:T(8,128)S(1)} fusion(f32[256,8,32,128]{3,2,1,0:T(8,128)} %bitcast.98, bf16[4096,2048]{0,1:T(8,128)(2,1)} %copy.59), kind=kLoop, calls=%fused_computation.48 | loop fusion | flops 16777216 | bytes 83886080 | tf_op jit(solution)/shard_map/add | solution.py:99
  877.2 11.7 copy-done
  890.2 66.0 %all-reduce.9.cloned.1.call-done = f32[512,512]{0,1:T(8,128)} async-done(((f32[512,512]{0,1:T(8,128)}), f32[512,512]{0,1:T(8,128)}) %all-reduce.9.cloned.1.call-update) | async-done | bytes 1048592 | tf_op jit(solution)/shard_map/psum | solution.py:12
  959.2 11.7 cholesky.103
  971.1 9.8 custom-call.33
  981.6 11.7 cholesky.212
  993.3 10.0 custom-call.34
  1003.9 11.7 cholesky.228
  1015.7 9.8 custom-call.35
  1026.1 12.3 cholesky.240
  1039.9 100.4 %conditional.1 = (f32[4096,512]{1,0:T(8,128)}) conditional(s32[]{:T(128)} %convert_element_type.23, () %tuple.39, (s32[]{:T(128)}, s32[4096,1]{0,1:T(1,128)S(1)}, s32[512,512]{0,1:T(8,128)S(1)}, s32[512,512]{0,1:T(8,128)S(1)}, s32[128,128]{1,0:T(8,128)S(1)}, /*index=5*/s32[128,128]{1,0:T(8,128)S(1)}, s32[128,128]{1,0:T(8,128)S(1)}, ...), branch_computations={%region_10.11_spmd, %region_11.20_spmd} | conditional | flops 8068735488 | bytes 104493288 | solution.py:111
  1049.5 3.0 fusion.15
  1052.5 12.2 while.1
  1053.2 2.2 dynamic-slice.7
  1064.7 39.5 %custom-call.29 = f32[4,128,128]{1,2,0:T(8,128)S(1)} custom-call(f32[4,128,128]{2,1,0:T(8,128)S(1)} %get-tuple-element.210), custom_call_target="InvertDiagBlocksLowerTriangular" | custom-call | tf_op jit(solution)/shard_map/cond/branch_1_fun/jit(_solve_triangular)/triangular_solve | solution.py:44
  1104.1 3.9 slice_bitcast_fusion
  1110.0 2.8 convolution_subtract_fusion.1
  1114.8 3.3 convolution_subtract_fusion
  1120.0 5.3 fusion.7
  1127.3 3.9 fusion
  1131.2 8.9 copy.79
  1140.3 7.8 broadcast_select_fusion.1
  1148.3 172.8 %all-reduce.11.cloned.1.call-done = f32[4096,512]{1,0:T(8,128)} async-done(((f32[4096,512]{1,0:T(8,128)}), f32[4096,512]{1,0:T(8,128)}) %all-reduce.11.cloned.1.call-update) | async-done | bytes 8388624 | tf_op jit(solution)/shard_map/psum | solution.py:12
  1321.1 5.8 broadcast_select_fusion.2
  1327.0 103.8 %all-reduce.13.cloned.1.call-done = bf16[4096,512]{1,0:T(8,128)(2,1)} async-done(((bf16[4096,512]{1,0:T(8,128)(2,1)}), bf16[4096,512]{1,0:T(8,128)(2,1)}) %all-reduce.13.cloned.1.call-update) | async-done | bytes 4194320 | tf_op jit(solution)/shard_map/psum | solution.py:12
  1430.8 29.4 %subtract_select_fusion = f32[4096,2048]{0,1:T(8,128)} fusion(f32[4096,2048]{0,1:T(8,128)} %copy-done, pred[4096]{0:T(1024)(128)(4,1)S(1)} %add_compare_fusion, pred[2048]{0:T(1024)(128)(4,1)S(1)} %add_compare_fusion.1, bf16[4096,512]{1,0:T(8,128)(2,1)} %all-reduce.13.cloned.1.call-done, s32[]{:T(128)S(6)} %select_n.218, ...), kind=kOutput, calls=%fused_computation.49 | convolution fusion | flops 8617197568 | bytes 77600768 | tf_op jit(solution)/shard_map/dot_general | solution.py:121
  1460.3 33.3 %copy.76 = f32[4096,2048]{1,0:T(8,128)} copy(f32[4096,2048]{0,1:T(8,128)} %subtract_select_fusion) | data formatting | bytes 67108864
  1493.6 7.8 copy.111
  (99 shorter events, 35.2 us)
Async XLA Ops:
  7.2 182.3 %all-reduce.7.cloned.1.call-start = ((), (), s32[]{:S(2)}) async-start(), calls=%async_computation.1 | async-start | bytes 16777216 | tf_op jit(solution)/shard_map/psum | solution.py:12
  14.5 0.7 copy-start.2
  345.7 363.4 %all-to-all-start = ((f32[32,512,256]{2,1,0:T(8,128)}), f32[32,512,256]{2,1,0:T(8,128)}, u32[]{:S(2)}, u32[]{:S(2)}) async-start(f32[32,512,256]{2,1,0:T(8,128)} %reshape.390), calls=%async_computation | async-start | bytes 33554432 | tf_op jit(solution)/shard_map/all_to_all | solution.py:83
  351.0 605.1 %all-reduce.9.cloned.1.call-start = ((), (), s32[]{:S(2)}) async-start(), calls=%async_computation.2 | async-start | bytes 2097152 | tf_op jit(solution)/shard_map/psum | solution.py:12
  877.1 11.7 copy-start
  889.9 431.2 %all-reduce.11.cloned.1.call-start = ((), (), s32[]{:S(2)}) async-start(), calls=%async_computation.3 | async-start | bytes 16777216 | tf_op jit(solution)/shard_map/psum | solution.py:12
  1015.7 22.8 %copy-start.1 = (f32[128,128]{1,0:T(8,128)}, f32[128,128]{1,0:T(8,128)S(1)}, u32[]{:S(2)}) copy-start(f32[128,128]{1,0:T(8,128)S(1)} %cholesky.228) | copy-start | bytes 196612
  1148.2 282.6 %all-reduce.13.cloned.1.call-start = ((), (), s32[]{:S(2)}) async-start(), calls=%async_computation.4 | async-start | bytes 8388608 | tf_op jit(solution)/shard_map/psum | solution.py:12
Sparse Core Ops, SparseCore 0:
  14.7 174.7 all-reduce.6
  890.1 66.0 all-reduce.8
  1148.3 172.7 all-reduce.10
  1327.1 103.7 all-reduce.12
where the time goes:
time: 1520 us; the launch traced here: 1510 us
  waiting for transfers between devices  834 us (55%)
  local copies, waits for them, and re-layouts  298 us (20%)
  other arithmetic  276 us (18%)
  matrix products  76.7 us (5%)
    psum x4, waiting for transfers between devices, broadcast(): return lax.psum(block, axis)  497 us
    all_to_all x1, waiting for transfers between devices, body(): lax.all_to_all(packed, ('cube', 'row', 'col'), split_axis=0, concat_axis=...  337 us
    unnamed x11, local copies, waits for them, and re-layouts  106 us
    another operation x16, other arithmetic, body(): local_factor = jnp.linalg.cholesky(pivot_block)  80 us
    scatter-add x1, other arithmetic, body(): jax.ops.segment_sum(pieces, targets.reshape(-1), num_segments=tiles_total)  51.6 us
    another operation x3, other arithmetic, solve_rows(): jax.scipy.linalg.solve_triangular(factor, raw_rows.T, lower=True)  42.5 us
    add x1, other arithmetic, body(): front_tile = parent_front.astype(jnp.float32) + assembled  37 us
    transpose x1, local copies, waits for them, and re-layouts, body(): assembled = summed.reshape(range_rows, range_cols, BLK, BLK).transpose(0,...  34.6 us
  transfers between devices with their start and end apart: 5, of which 5 were waited for; matrix products, arithmetic and copies ran while one was open for 3% of the time, Pallas kernels for 0%

commit v1 on v0

v1 whole, which is shorter than its diff:
```python
import functools

import jax
import jax.numpy as jnp
from jax import lax
from jax.experimental import pallas as pl
from jax.experimental.pallas import tpu as pltpu
from jax.sharding import PartitionSpec as P

BLK = 128
PANEL = 512
WIRE = jnp.float16
SHRINK = 1.0 / 4.0
FRONT_SHRINK = 1.0 / 8.0
HIGHEST = lax.Precision.HIGHEST


def group_ranks(labels):
    position = jnp.arange(labels.shape[-1])
    before = position[:, None] > position[None, :]
    same_label = labels[..., :, None] == labels[..., None, :]
    return jnp.sum(jnp.logical_and(same_label, before), axis=-1)


def member_of_slot(slot, slots, count):
    hits = (slot[:, None] == jnp.arange(slots)).astype(jnp.int32)
    return jnp.sum(hits * jnp.arange(count, dtype=jnp.int32)[:, None], axis=0)


def slot_of_block(grouped, slot_in_group, cap, first, count):
    groups = grouped.shape[1]
    wanted = first + jnp.arange(count, dtype=jnp.int32)
    hits = grouped[..., None] == wanted
    value = jnp.arange(groups, dtype=jnp.int32)[None, :, None] * cap + slot_in_group
    total = jnp.sum(jnp.where(hits, value[..., None] + 1, 0), axis=(1, 2))
    return total.astype(jnp.int32) - 1


def pack_kernel(slots, tables, rows_ref, panel_ref, update_ref, out_ref, held):
    cubes, cols, cap = slots
    product = lax.dot_general(
        rows_ref[...], panel_ref[...], (((1,), (1,)), ((), ())), preferred_element_type=jnp.float32
    )
    held[...] = (update_ref[...] - product) * SHRINK
    count = pl.num_programs(0)
    for cube in range(cubes):
        for col in range(cols):
            for rank in range(cap):
                slot = (cube * cols + col) * cap + rank
                start = pl.multiple_of(tables[count + slot] * BLK, BLK)
                out_ref[cube, 0, col, :, rank * BLK : (rank + 1) * BLK] = held[
                    :, pl.ds(start, BLK)
                ]


def pack(own_panel, column_panel, update, my_rows, my_cols, sizes):
    cubes, rows, cols, row_cap, col_cap = sizes
    group_blocks = update.shape[0] // BLK
    width = update.shape[1]
    depth = own_panel.shape[1]
    tables = jnp.concatenate([my_rows, my_cols]).astype(jnp.int32)
    return pl.pallas_call(
        functools.partial(pack_kernel, (cubes, cols, col_cap)),
        out_shape=jax.ShapeDtypeStruct(
            (cubes, rows, cols, row_cap * BLK, col_cap * BLK), jnp.float32
        ),
        grid_spec=pltpu.PrefetchScalarGridSpec(
            num_scalar_prefetch=1,
            grid=(group_blocks,),
            in_specs=[
                pl.BlockSpec((BLK, depth), lambda s, t: (t[s], 0)),
                pl.BlockSpec((width, depth), lambda s, t: (0, 0)),
                pl.BlockSpec((BLK, width), lambda s, t: (t[s], 0)),
            ],
            out_specs=pl.BlockSpec(
                (cubes, 1, cols, BLK, col_cap * BLK),
                lambda s, t: (0, s // row_cap, 0, s % row_cap, 0),
            ),
            scratch_shapes=[pltpu.VMEM((BLK, width), jnp.float32)],
        ),
        compiler_params=pltpu.CompilerParams(vmem_limit_bytes=50 * 2**20),
        name="pack",
    )(tables, own_panel, column_panel, update)


def front_block(tables, layout, parent_ref, arrived, block):
    range_rows, range_cols, col_cap = layout
    children = len(arrived)
    step = pl.program_id(0)
    total = parent_ref[:, block * BLK : (block + 1) * BLK].astype(jnp.float32)
    for child, ref in enumerate(arrived):
        row_slot = tables[child * range_rows + step]
        col_slot = tables[children * range_rows + child * range_cols + block]
        slot = jnp.maximum(col_slot, 0)
        start = pl.multiple_of((slot % col_cap) * BLK, BLK)
        piece = ref[0, 0, slot // col_cap, :, pl.ds(start, BLK)]
        factor = jnp.where((row_slot >= 0) & (col_slot >= 0), 1.0 / SHRINK, 0.0)
        total = total + piece * factor
    return total


def strip_kernel(layout, blocks, tables, parent_ref, *refs):
    arrived, out_ref = refs[:-1], refs[-1]
    for block in range(blocks):
        out_ref[:, block * BLK : (block + 1) * BLK] = front_block(
            tables, layout, parent_ref, arrived, block
        )


def final_kernel(layout, blocks, tables, parent_ref, rows_ref, cols_ref, *refs):
    arrived, out_ref = refs[:-1], refs[-1]
    range_rows, range_cols, col_cap = layout
    children = len(arrived)
    base = children * (range_rows + range_cols)
    first_row, first_col = tables[base], tables[base + 1]
    row_ok = first_row + pl.program_id(0) >= PANEL // BLK
    product = jnp.dot(rows_ref[...], cols_ref[...], preferred_element_type=jnp.float32)
    for block in range(blocks):
        total = front_block(tables, layout, parent_ref, arrived, block)
        keep = row_ok & (first_col + block >= PANEL // BLK)
        left = total - product[:, block * BLK : (block + 1) * BLK]
        out_ref[:, block * BLK : (block + 1) * BLK] = jnp.where(keep, left, 0.0)


def over_front(kernel, name, tables, parent, arrived, extras, extra_specs, row_blocks, col_blocks):
    children, rows, cols, high, wide = arrived.shape
    row_cap, col_cap = high // BLK, wide // BLK
    range_rows, range_cols = parent.shape[0] // BLK, parent.shape[1] // BLK
    width = col_blocks * BLK

    def source(child):
        def index(step, t):
            slot = jnp.maximum(t[child * range_rows + step], 0)
            return (child, slot // row_cap, 0, slot % row_cap, 0)

        return pl.BlockSpec((1, 1, cols, BLK, wide), index)

    return pl.pallas_call(
        functools.partial(kernel, (range_rows, range_cols, col_cap), col_blocks),
        out_shape=jax.ShapeDtypeStruct((row_blocks * BLK, width), jnp.float32),
        grid_spec=pltpu.PrefetchScalarGridSpec(
            num_scalar_prefetch=1,
            grid=(row_blocks,),
            in_specs=[pl.BlockSpec((BLK, width), lambda s, t: (s, 0))]
            + extra_specs
            + [source(child) for child in range(children)],
            out_specs=pl.BlockSpec((BLK, width), lambda s, t: (s, 0)),
        ),
        compiler_params=pltpu.CompilerParams(vmem_limit_bytes=50 * 2**20),
        name=name,
    )(tables, parent, *extras, *([arrived] * children))


def factor_pivot(pivot):
    steps = PANEL // BLK
    left = [
        [pivot[i * BLK : (i + 1) * BLK, j * BLK : (j + 1) * BLK] for j in range(i + 1)]
        for i in range(steps)
    ]
    factor = [[None] * steps for _ in range(steps)]
    inverses = []
    unit = jnp.eye(BLK, dtype=jnp.float32)
    for j in range(steps):
        factor[j][j] = jnp.linalg.cholesky(left[j][j], symmetrize_input=False)
        inverse = jax.scipy.linalg.solve_triangular(factor[j][j], unit, lower=True)
        inverses.append(inverse)
        for i in range(j + 1, steps):
            factor[i][j] = jnp.dot(left[i][j], inverse.T, precision=HIGHEST)
        for i in range(j + 1, steps):
            for m in range(j + 1, i + 1):
                left[i][m] = left[i][m] - jnp.dot(factor[i][j], factor[m][j].T, precision=HIGHEST)
    return factor, inverses


def solve_cols(factor, inverses, top):
    done = []
    for j in range(PANEL // BLK):
        right = top[j * BLK : (j + 1) * BLK]
        if j:
            known = jnp.concatenate(factor[j][:j], axis=1)
            right = right - jnp.dot(known, jnp.concatenate(done, axis=0), precision=HIGHEST)
        done.append(jnp.dot(inverses[j], right, precision=HIGHEST))
    return jnp.concatenate(done, axis=0)


def solve_rows(factor, inverses, strip):
    done = []
    for j in range(PANEL // BLK):
        right = strip[:, j * BLK : (j + 1) * BLK]
        if j:
            known = jnp.concatenate(factor[j][:j], axis=1)
            right = right - jnp.dot(jnp.concatenate(done, axis=1), known.T, precision=HIGHEST)
        done.append(jnp.dot(right, inverses[j].T, precision=HIGHEST))
    return jnp.concatenate(done, axis=1)


def body(child_update, child_panel, parent_front, block_map):
    grid_rows = lax.axis_size("row")
    cube_count = lax.axis_size("cube")
    col_count = lax.axis_size("col")
    grid_cols = cube_count * col_count
    child_index = lax.axis_index("cube")
    row_index = lax.axis_index("row")
    col_index = lax.axis_index("col")
    range_index = lax.axis_index(("cube", "col"))
    group_blocks = child_update.shape[1] // BLK
    row_cap = group_blocks // grid_rows
    col_cap = max(1, group_blocks // grid_cols)
    front_rows, front_cols = parent_front.shape
    range_rows = front_rows // BLK
    range_cols = front_cols // BLK

    own_panel = child_panel[0]
    share = own_panel.shape[0] // col_count
    piece = lax.dynamic_slice_in_dim(own_panel, col_index * share, share, 0)
    swap = [
        (r * col_count + c, c * col_count + r) for r in range(grid_rows) for c in range(col_count)
    ]
    piece = lax.ppermute(piece, ("row", "col"), swap)
    column_panel = lax.all_gather(piece, "row", axis=0, tiled=True)

    children = block_map.shape[0]
    grouped = block_map.reshape(children, grid_rows, group_blocks)
    row_dest = grouped // range_rows
    col_dest = grouped // range_cols
    row_slot = row_dest * row_cap + group_ranks(row_dest)
    col_rank = group_ranks(col_dest)
    row_rank = row_slot - row_dest * row_cap
    col_slot = col_dest * col_cap + col_rank
    my_rows = member_of_slot(row_slot[child_index, row_index], group_blocks, group_blocks)
    my_cols = member_of_slot(col_slot[child_index, col_index], grid_cols * col_cap, group_blocks)
    from_rows = slot_of_block(grouped, row_rank, row_cap, row_index * range_rows, range_rows)
    from_cols = slot_of_block(grouped, col_rank, col_cap, range_index * range_cols, range_cols)
    tables = jnp.concatenate(
        [
            from_rows.reshape(-1),
            from_cols.reshape(-1),
            jnp.stack([row_index * range_rows, range_index * range_cols]),
        ]
    ).astype(jnp.int32)

    packed = pack(
        own_panel,
        column_panel,
        child_update[0],
        my_rows,
        my_cols,
        (cube_count, grid_rows, col_count, row_cap, col_cap),
    )
    shape = packed.shape
    packed = packed.astype(WIRE)
    arrived = lax.all_to_all(
        packed.reshape((-1,) + shape[3:]),
        ("cube", "row", "col"),
        split_axis=0,
        concat_axis=0,
        tiled=True,
    )
    arrived = arrived.astype(jnp.float32).reshape(shape)

    panel_blocks = PANEL // BLK
    strip = over_front(
        strip_kernel, "strip", tables, parent_front, arrived, [], [], range_rows, panel_blocks
    )
    top = over_front(
        strip_kernel, "top", tables, parent_front, arrived, [], [], panel_blocks, range_cols
    )
    corner = (row_index == 0) & (range_index == 0)
    pivot = lax.psum(jnp.where(corner, strip[:PANEL], 0.0), ("cube", "row", "col"))
    top_low = jnp.where(row_index == 0, top * FRONT_SHRINK, 0.0).astype(WIRE)
    strip_low = jnp.where(range_index == 0, strip * FRONT_SHRINK, 0.0).astype(WIRE)
    top_all = lax.psum(top_low, "row").astype(jnp.float32) * (1.0 / FRONT_SHRINK)
    strip_all = lax.psum(strip_low, ("cube", "col")).astype(jnp.float32) * (1.0 / FRONT_SHRINK)

    factor, inverses = factor_pivot(pivot)
    cols_low = solve_cols(factor, inverses, top_all).astype(jnp.bfloat16)
    solved = solve_rows(factor, inverses, strip_all)
    zero = jnp.zeros((BLK, BLK), jnp.float32)
    lower = jnp.concatenate(
        [
            jnp.concatenate(
                [factor[i][j] if j <= i else zero for j in range(panel_blocks)], axis=1
            )
            for i in range(panel_blocks)
        ],
        axis=0,
    )
    head = jnp.where(row_index == 0, lower, solved[:PANEL])
    panel_rows = lax.dynamic_update_slice(solved, head, (0, 0))
    rows_low = panel_rows.astype(jnp.bfloat16)
    schur = over_front(
        final_kernel,
        "final",
        tables,
        parent_front,
        arrived,
        [rows_low, cols_low],
        [
            pl.BlockSpec((BLK, PANEL), lambda s, t: (s, 0)),
            pl.BlockSpec((PANEL, front_cols), lambda s, t: (0, 0)),
        ],
        range_rows,
        range_cols,
    )
    return (schur, panel_rows)


def solution(mesh):
    placed = (P("cube", "row", "col"), P("cube", "row", None), P("row", ("cube", "col")), P())
    return jax.shard_map(
        body,
        mesh=mesh,
        in_specs=placed,
        out_specs=(P("row", ("cube", "col")), P("row", None)),
        check_vma=False,
    )
```

time: 1520 us -> 1150 us (0.76)
  waiting for transfers between devices: 834 us -> 529 us
  local copies, waits for them, and re-layouts: 298 us -> 15.8 us
  blocking collectives: 0 us -> 244 us
  other arithmetic: 276 us -> 136 us
  Pallas kernels: 0 us -> 127 us
    psum x4 -> x1, waiting for transfers between devices: 497 us -> 121 us  [body(): lax.psum(jnp.where(corner, strip[:PANEL], 0.0), ('cube', 'row', 'col'))]
    psum x0 -> x2, blocking collectives: none -> 244 us  [the longest x1 171 us: body(): lax.psum(strip_low, ('cube', 'col')).astype(jnp.float32)]
    all_gather x0 -> x1, waiting for transfers between devices: none -> 228 us  [body(): column_panel = lax.all_gather(piece, 'row', axis=0, tiled=True)]
    all_to_all x1, waiting for transfers between devices: 337 us -> 180 us  [body(): lax.all_to_all(packed.reshape((-1,) + shape[3:]), ('cube', 'row', 'col'),...]
    pallas_call x0 -> x4, Pallas kernels: none -> 127 us  [the longest x3 72.5 us: over_front(): pl.pallas_call(functools.partial(kernel, (range_rows, range_cols, col_cap...]
    unnamed x11 -> x22, local copies, waits for them, and re-layouts: 106 us -> 5.78 us
    reshape x4 -> x0, local copies, waits for them, and re-layouts: 63.9 us -> none  [the longest x1 21.6 us: body(): packed.transpose(3, 0, 4, 1, 2, 5, 6)]
    scatter-add x1 -> x0, other arithmetic: 51.6 us -> none  [body(): jax.ops.segment_sum(pieces, targets.reshape(-1), num_segments=tiles_total)]
  transfers between devices with their start and end apart: 5 -> 4, of which waited for: 5 -> 3; matrix products, arithmetic and copies ran while one was open for 3% -> 1% of each run, Pallas kernels for 0% -> 0%
where the time goes in v1:
time: 1150 us; the launch traced here: 1140 us
  waiting for transfers between devices  529 us (46%)
  blocking collectives  244 us (21%)
  other arithmetic  136 us (12%)
  Pallas kernels  127 us (11%)
  matrix products  65.9 us (6%)
  local copies, waits for them, and re-layouts  15.8 us (1%)
  between operations  14.9 us (1%)
    all_gather x1, waiting for transfers between devices, body(): column_panel = lax.all_gather(piece, 'row', axis=0, tiled=True)  228 us
    all_to_all x1, waiting for transfers between devices, body(): lax.all_to_all(packed.reshape((-1,) + shape[3:]), ('cube', 'row', 'col'),...  180 us
    psum x1, blocking collectives, body(): lax.psum(strip_low, ('cube', 'col')).astype(jnp.float32)  171 us
    psum x1, waiting for transfers between devices, body(): lax.psum(jnp.where(corner, strip[:PANEL], 0.0), ('cube', 'row', 'col'))  121 us
    psum x1, blocking collectives, body(): lax.psum(top_low, 'row').astype(jnp.float32) * (1.0 / FRONT_SHRINK)  73.2 us
    pallas_call x3, Pallas kernels, over_front(): pl.pallas_call(functools.partial(kernel, (range_rows, range_cols, col_cap...  72.5 us
    pallas_call x1, Pallas kernels, pack(): pl.pallas_call(functools.partial(pack_kernel, (cubes, cols, col_cap)), ou...  54.2 us
    another operation x12, other arithmetic, factor_pivot(): factor[j][j] = jnp.linalg.cholesky(left[j][j], symmetrize_input=False)  49.7 us
  transfers between devices with their start and end apart: 4, of which 3 were waited for; matrix products, arithmetic and copies ran while one was open for 1% of the time, Pallas kernels for 0%

profile of v1, /device:TPU:0, one launch (start us, length us, event | category | flops | bytes accessed | tf_op | source)
XLA Modules:
  0.0 1138.5 jit_solution(18364731213839874622)
XLA Ops:
  7.2 1.7 dynamic-slice_bitcast_fusion
  9.8 1.3 copy-done.9
  11.9 227.9 %all-gather.2.cloned.1.call-done.panel_ref = bf16[2048,2048]{1,0:T(8,128)(2,1)} async-done(((bf16[512,2048]{1,0:T(8,128)(2,1)}), bf16[2048,2048]{1,0:T(8,128)(2,1)}) %all-gather.2.cloned.1.call-update) | async-done | bytes 8388624 | tf_op jit(solution)/shard_map/all_gather | solution.py:220
  239.8 54.2 %pack.1 = f32[2,4,4,512,256]{4,3,2,1,0:T(8,128)} custom-call(s32[32]{0:T(128)S(1)} %pad_add_fusion.1.tables, bf16[2048,2048]{1,0:T(8,128)(2,1)} %bitcast.88, bf16[2048,2048]{1,0:T(8,128)(2,1)} %all-gather.2.cloned.1.call-done.panel_ref, f32[2048,2048]{1,0:T(8,128)} %bitcast.86), custom_call_target="tpu_custom_call" | custom-call | tf_op jit(solution)/shard_map/pack/pallas_call | solution.py:62
  293.9 9.0 convert_element_type.39
  302.9 4.7 all-to-all-start
  308.3 180.3 %all-to-all-done = f16[32,512,256]{2,1,0:T(8,128)(2,1)} async-done(((f16[32,512,256]{2,1,0:T(8,128)(2,1)}), f16[32,512,256]{2,1,0:T(8,128)(2,1)}, u32[]{:S(2)}, u32[]{:S(2)}) %all-to-all-start) | async-done | bytes 8388640 | tf_op jit(solution)/shard_map/all_to_all | solution.py:252
  488.7 10.7 convert.17.refs_0_.refs_1_
  499.3 6.1 top.1
  505.4 25.0 %strip.1 = f32[4096,512]{1,0:T(8,128)} custom-call(s32[98]{0:T(128)S(1)} %pad_add_fusion.tables, bf16[4096,2048]{1,0:T(8,128)(2,1)} %parent_ref.5, f32[2,4,4,512,256]{4,3,2,1,0:T(8,128)} %convert.17.refs_0_.refs_1_, f32[2,4,4,512,256]{4,3,2,1,0:T(8,128)} %convert.17.refs_0_.refs_1_), custom_call_target="tpu_custom_call" | custom-call | tf_op jit(solution)/shard_map/strip/pallas_call | solution.py:138
  530.4 1.9 select_convert_fusion.1
  532.3 73.2 %all-reduce.6 = u32[4,131072]{1,0:T(4,128)S(1)} all-reduce(u32[4,131072]{1,0:T(4,128)} %bitcast.90), channel_id=1, replica_groups=mesh['cube'=2,'row'=4,'col'=4] {'row'}, use_global_device_ids=true, to_apply=%region_10.13.clone | all-reduce | flops 524288 | bytes 4194304 | tf_op jit(solution)/shard_map/psum | solution.py:272
  605.5 6.6 select_convert_fusion
  612.1 2.3 slice_select_fusion.1
  614.4 170.9 %all-reduce.7 = u32[4,262144]{1,0:T(4,128)} all-reduce(u32[4,262144]{1,0:T(4,128)} %bitcast.87), channel_id=1, replica_groups=mesh['cube'=2,'row'=4,'col'=4] {'cube','col'}, use_global_device_ids=true, to_apply=%region_6.7.clone | all-reduce | flops 1048576 | bytes 8388608 | tf_op jit(solution)/shard_map/psum | solution.py:273
  785.4 6.7 convert_multiply_fusion
  792.2 2.5 convert_multiply_fusion.1
  794.7 121.1 %all-reduce.5.cloned.1.call-done = f32[512,512]{1,0:T(8,128)} async-done(((f32[512,512]{1,0:T(8,128)}), f32[512,512]{1,0:T(8,128)}) %all-reduce.5.cloned.1.call-update) | async-done | bytes 1048592 | tf_op jit(solution)/shard_map/psum | solution.py:269
  916.6 11.7 %cholesky.75 = f32[128,128]{1,0:T(8,128)S(1)} custom-call(f32[128,128]{1,0:T(8,128)S(1)} %slice.90), custom_call_target="Cholesky" | custom-call | tf_op jit(solution)/shard_map/jit(cholesky)/cholesky | solution.py:164
  929.6 9.8 custom-call.8
  940.9 3.6 fusion.21
  944.5 6.1 convolution_subtract_fusion.1
  950.6 1.9 copy.16
  953.6 11.7 %cholesky.86 = f32[128,128]{1,0:T(8,128)S(1)} custom-call(f32[128,128]{1,0:T(8,128)S(1)} %convolution_subtract_fusion.13), custom_call_target="Cholesky" | custom-call | tf_op jit(solution)/shard_map/jit(cholesky)/cholesky | solution.py:164
  966.6 9.8 custom-call.9
  977.9 1.1 convolution_subtract_fusion.12
  979.4 3.6 fusion.66
  983.0 1.3 copy-done.1
  984.3 9.8 convolution_subtract_fusion
  994.2 2.9 copy.17
  998.3 1.1 convolution_subtract_fusion.9
  999.8 1.1 convolution_subtract_fusion.8
  1002.6 11.7 %cholesky.97 = f32[128,128]{1,0:T(8,128)S(1)} custom-call(f32[128,128]{1,0:T(8,128)S(1)} %convolution_subtract_fusion.10), custom_call_target="Cholesky" | custom-call | tf_op jit(solution)/shard_map/jit(cholesky)/cholesky | solution.py:164
  1015.8 9.8 custom-call.10
  1026.3 3.7 fusion.68
  1030.0 1.3 copy-done.3
  1031.3 12.9 %fusion.6 = f32[4096,128]{1,0:T(8,128)} fusion(f32[4096,128]{0,1:T(8,128)S(1)} %fusion.68, f32[4096,128]{0,1:T(8,128)S(1)} %copy-done.2, f32[4096,128]{0,1:T(8,128)S(1)} %fusion.21, f32[4096,512]{1,0:T(8,128)} %convert_multiply_fusion, f32[128,128]{0,1:T(8,128)S(1)} %fusion.70, f32[128,128]{0,1:T(8,128)S(1)} %fusion.69, f32[128,128]{0,1:T(8,128)S(1)} %fusion.39), kind=kOutput, calls=%fused_computation.11 | convolution fusion | flops 2419687424 | bytes 10682368 | tf_op jit(solution)/shard_map/dot_general | solution.py:192
  1044.2 1.9 copy.18
  1047.8 11.7 %cholesky.108 = f32[128,128]{1,0:T(8,128)S(1)} custom-call(f32[128,128]{1,0:T(8,128)S(1)} %convolution_subtract_fusion.4), custom_call_target="Cholesky" | custom-call | tf_op jit(solution)/shard_map/jit(cholesky)/cholesky | solution.py:164
  1060.9 9.8 custom-call.11
  1071.0 2.2 fusion.65
  1073.2 2.5 convolution_subtract_fusion.3
  1076.7 1.3 convolution_subtract_fusion.2
  1079.0 2.3 fusion.18
  1082.4 1.9 fusion.71
  1085.2 2.9 convert_element_type.43.rows_ref
  1088.0 1.8 copy-done
  1090.0 41.4 %final.1 = f32[4096,2048]{1,0:T(8,128)} custom-call(s32[98]{0:T(128)S(1)} %pad_add_fusion.tables, bf16[4096,2048]{1,0:T(8,128)(2,1)} %parent_ref.5, bf16[4096,512]{1,0:T(8,128)(2,1)} %convert_element_type.43.rows_ref, bf16[512,2048]{1,0:T(8,128)(2,1)S(1)} %pad_maximum_fusion.1.cols_ref, f32[2,4,4,512,256]{4,3,2,1,0:T(8,128)} %convert.17.refs_0_.refs_1_, ...), custom_call_target="tpu_custom_call" | custom-call | tf_op jit(solution)/shard_map/final/pallas_call | solution.py:138
  (88 shorter events, 22.9 us)
Async XLA Ops:
  7.2 232.6 %all-gather.2.cloned.1.call-start = ((), (), s32[]{:S(2)}) async-start(), calls=%async_computation.1 | async-start | bytes 10485760 | tf_op jit(solution)/shard_map/all_gather | solution.py:220
  7.2 3.9 copy-start.10
  9.0 0.8 collective-permute-start
  9.8 1.3 copy-start.9
  302.9 185.7 %all-to-all-start = ((f16[32,512,256]{2,1,0:T(8,128)(2,1)}), f16[32,512,256]{2,1,0:T(8,128)(2,1)}, u32[]{:S(2)}, u32[]{:S(2)}) async-start(f16[32,512,256]{2,1,0:T(8,128)(2,1)} %bitcast.84), calls=%async_computation | async-start | bytes 16777216 | tf_op jit(solution)/shard_map/all_to_all | solution.py:252
  307.7 608.1 %all-reduce.5.cloned.1.call-start = ((), (), s32[]{:S(2)}) async-start(), calls=%async_computation.2 | async-start | bytes 2097152 | tf_op jit(solution)/shard_map/psum | solution.py:269
  505.4 25.0 %copy-start.5 = (f32[512,2048]{1,0:T(8,128)S(1)}, f32[512,2048]{1,0:T(8,128)}, u32[]{:S(2)}) copy-start(f32[512,2048]{1,0:T(8,128)} %top.1) | copy-start | bytes 12582916
  983.0 1.3 copy-start.1
  1026.3 5.1 copy-start.2
  1030.0 1.3 copy-start.3
  1073.2 3.5 copy-start.4
  1079.0 3.3 copy-start.6
  1081.3 2.9 copy-start.7
  1081.3 2.9 copy-start.8
  1085.1 4.7 copy-start
Sparse Core Ops, SparseCore 0:
  11.2 228.4 all-gather.1
  785.5 130.2 all-reduce.4

commit v2 on v1

--- a/solution.py
+++ b/solution.py
@@ -34,6 +34,19 @@
     value = jnp.arange(groups, dtype=jnp.int32)[None, :, None] * cap + slot_in_group
     total = jnp.sum(jnp.where(hits, value[..., None] + 1, 0), axis=(1, 2))
     return total.astype(jnp.int32) - 1
+
+
+def spread(block, axes):
+    count = lax.axis_size(axes)
+    copies = jnp.broadcast_to(block[None], (count,) + block.shape)
+    joined = lax.all_to_all(copies, axes, split_axis=0, concat_axis=0, tiled=True)
+    return joined.reshape((-1,) + block.shape[1:])
+
+
+def broadcast(block, axes):
+    count = lax.axis_size(axes)
+    shares = block.reshape((count, -1) + block.shape[1:])
+    return spread(lax.all_to_all(shares, axes, split_axis=0, concat_axis=0, tiled=True)[0], axes)
 
 
 def pack_kernel(slots, tables, rows_ref, panel_ref, update_ref, out_ref, held):
@@ -217,7 +230,7 @@
         (r * col_count + c, c * col_count + r) for r in range(grid_rows) for c in range(col_count)
     ]
     piece = lax.ppermute(piece, ("row", "col"), swap)
-    column_panel = lax.all_gather(piece, "row", axis=0, tiled=True)
+    column_panel = spread(piece, "row")
 
     children = block_map.shape[0]
     grouped = block_map.reshape(children, grid_rows, group_blocks)
@@ -265,12 +278,12 @@
     top = over_front(
         strip_kernel, "top", tables, parent_front, arrived, [], [], panel_blocks, range_cols
     )
-    corner = (row_index == 0) & (range_index == 0)
-    pivot = lax.psum(jnp.where(corner, strip[:PANEL], 0.0), ("cube", "row", "col"))
-    top_low = jnp.where(row_index == 0, top * FRONT_SHRINK, 0.0).astype(WIRE)
-    strip_low = jnp.where(range_index == 0, strip * FRONT_SHRINK, 0.0).astype(WIRE)
-    top_all = lax.psum(top_low, "row").astype(jnp.float32) * (1.0 / FRONT_SHRINK)
-    strip_all = lax.psum(strip_low, ("cube", "col")).astype(jnp.float32) * (1.0 / FRONT_SHRINK)
+    pivot = broadcast(strip[:PANEL], ("cube", "row", "col"))
+    top_low, strip_low, pivot = lax.optimization_barrier(
+        ((top * FRONT_SHRINK).astype(WIRE), (strip * FRONT_SHRINK).astype(WIRE), pivot)
+    )
+    top_all = broadcast(top_low, "row").astype(jnp.float32) * (1.0 / FRONT_SHRINK)
+    strip_all = broadcast(strip_low, ("cube", "col")).astype(jnp.float32) * (1.0 / FRONT_SHRINK)
 
     factor, inverses = factor_pivot(pivot)
     cols_low = solve_cols(factor, inverses, top_all).astype(jnp.bfloat16)

time: 1150 us -> 974 us (0.85)
  blocking collectives: 244 us -> 62.7 us
  starting transfers between devices: 5.59 us -> 166 us
  waiting for transfers between devices: 529 us -> 376 us
  local copies, waits for them, and re-layouts: 15.8 us -> 37.8 us
  between operations: 14.9 us -> 1.81 us
    psum x2 -> x0, blocking collectives: 244 us -> none  [the longest x1 171 us: body(): lax.psum(strip_low, ('cube', 'col')).astype(jnp.float32)]
    all_gather x1 -> x0, waiting for transfers between devices: 228 us -> none  [body(): column_panel = lax.all_gather(piece, 'row', axis=0, tiled=True)]
    all_to_all x0 -> x5, waiting for transfers between devices: none -> 196 us  [the longest x4 127 us: spread(): lax.all_to_all(copies, axes, split_axis=0, concat_axis=0, tiled=True)]
    all_to_all x0 -> x5, starting transfers between devices: none -> 160 us  [the longest x4 155 us: spread(): lax.all_to_all(copies, axes, split_axis=0, concat_axis=0, tiled=True)]
    psum x1 -> x0, waiting for transfers between devices: 121 us -> none  [body(): lax.psum(jnp.where(corner, strip[:PANEL], 0.0), ('cube', 'row', 'col'))]
    all_to_all x0 -> x2, blocking collectives: none -> 62.7 us  [broadcast(): lax.all_to_all(shares, axes, split_axis=0, concat_axis=0, tiled=True)[0]]
    broadcast_in_dim x0 -> x7, local copies, waits for them, and re-layouts: none -> 13.7 us  [spread(): copies = jnp.broadcast_to(block[None], (count,) + block.shape)]
  transfers between devices with their start and end apart: 4 -> 7, of which waited for: 3 -> 5; matrix products, arithmetic and copies ran while one was open for 1% -> 14% of each run, Pallas kernels for 0% -> 1%
where the time goes in v2:
time: 974 us; the launch traced here: 963 us
  waiting for transfers between devices  376 us (39%)
  starting transfers between devices  166 us (17%)
  other arithmetic  138 us (14%)
  Pallas kernels  126 us (13%)
  blocking collectives  62.7 us (6%)
  matrix products  55.2 us (6%)
  local copies, waits for them, and re-layouts  37.8 us (4%)
    all_to_all x1, waiting for transfers between devices, body(): lax.all_to_all(packed.reshape((-1,) + shape[3:]), ('cube', 'row', 'col'),...  180 us
    all_to_all x4, starting transfers between devices, spread(): lax.all_to_all(copies, axes, split_axis=0, concat_axis=0, tiled=True)  155 us
    all_to_all x4, waiting for transfers between devices, spread(): lax.all_to_all(copies, axes, split_axis=0, concat_axis=0, tiled=True)  127 us
    pallas_call x3, Pallas kernels, over_front(): pl.pallas_call(functools.partial(kernel, (range_rows, range_cols, col_cap...  71.8 us
    all_to_all x1, waiting for transfers between devices, broadcast(): lax.all_to_all(shares, axes, split_axis=0, concat_axis=0, tiled=True)[0]  68.8 us
    all_to_all x2, blocking collectives, broadcast(): lax.all_to_all(shares, axes, split_axis=0, concat_axis=0, tiled=True)[0]  62.7 us
    pallas_call x1, Pallas kernels, pack(): pl.pallas_call(functools.partial(pack_kernel, (cubes, cols, col_cap)), ou...  54.2 us
    another operation x12, other arithmetic, factor_pivot(): factor[j][j] = jnp.linalg.cholesky(left[j][j], symmetrize_input=False)  52 us
  transfers between devices with their start and end apart: 7, of which 5 were waited for; matrix products, arithmetic and copies ran while one was open for 14% of the time, Pallas kernels for 1%

profile of v2, /device:TPU:0, one launch (start us, length us, event | category | flops | bytes accessed | tf_op | source)
XLA Modules:
  0.0 963.2 jit_solution(13694044113846635914)
XLA Ops:
  3.2 4.5 broadcast_in_dim.44
  7.6 143.6 %all-to-all-start = ((bf16[4,512,2048]{2,1,0:T(8,128)(2,1)}), bf16[4,512,2048]{2,1,0:T(8,128)(2,1)}, u32[]{:S(2)}, u32[]{:S(2)}) async-start(bf16[4,512,2048]{2,1,0:T(8,128)(2,1)} %broadcast_in_dim.44), calls=%async_computation | async-start | bytes 16777216 | tf_op jit(solution)/shard_map/all_to_all | solution.py:42
  152.0 93.7 %all-to-all-done = bf16[4,512,2048]{2,1,0:T(8,128)(2,1)} async-done(((bf16[4,512,2048]{2,1,0:T(8,128)(2,1)}), bf16[4,512,2048]{2,1,0:T(8,128)(2,1)}, u32[]{:S(2)}, u32[]{:S(2)}) %all-to-all-start) | async-done | bytes 8388640 | tf_op jit(solution)/shard_map/all_to_all | solution.py:42
  245.7 54.2 %pack.1 = f32[2,4,4,512,256]{4,3,2,1,0:T(8,128)} custom-call(s32[32]{0:T(128)S(1)} %pad_add_fusion.1.tables, bf16[2048,2048]{1,0:T(8,128)(2,1)} %bitcast.116, bf16[2048,2048]{1,0:T(8,128)(2,1)} %bitcast.6.panel_ref, f32[2048,2048]{1,0:T(8,128)} %bitcast.115), custom_call_target="tpu_custom_call" | custom-call | tf_op jit(solution)/shard_map/pack/pallas_call | solution.py:75
  299.9 9.0 convert_element_type.41
  308.9 5.0 all-to-all-start.1
  314.6 180.4 %all-to-all-done.1 = f16[32,512,256]{2,1,0:T(8,128)(2,1)} async-done(((f16[32,512,256]{2,1,0:T(8,128)(2,1)}), f16[32,512,256]{2,1,0:T(8,128)(2,1)}, u32[]{:S(2)}, u32[]{:S(2)}) %all-to-all-start.1) | async-done | bytes 8388640 | tf_op jit(solution)/shard_map/all_to_all | solution.py:265
  494.9 10.7 %convert.17.refs_0_.refs_1_ = f32[2,4,4,512,256]{4,3,2,1,0:T(8,128)} convert(f16[2,4,4,512,256]{4,3,2,1,0:T(8,128)(2,1)} %bitcast.10) | non-fusion elementwise | flops 4194304 | bytes 25165824 | tf_op jit(solution)/shard_map/reshape | solution.py:272
  505.6 24.6 %strip.1 = f32[4096,512]{1,0:T(8,128)} custom-call(s32[98]{0:T(128)S(1)} %pad_add_fusion.tables, bf16[4096,2048]{1,0:T(8,128)(2,1)} %parent_ref.5, f32[2,4,4,512,256]{4,3,2,1,0:T(8,128)} %convert.17.refs_0_.refs_1_, f32[2,4,4,512,256]{4,3,2,1,0:T(8,128)} %convert.17.refs_0_.refs_1_), custom_call_target="tpu_custom_call" | custom-call | tf_op jit(solution)/shard_map/strip/pallas_call | solution.py:151
  531.5 34.5 %all_to_all.40 = f32[32,16,512]{2,1,0:T(8,128)S(1)} all-to-all(f32[32,16,512]{2,1,0:T(8,128)S(1)} %bitcast.118), channel_id=1, replica_groups=mesh['cube'=2,'row'=4,'col'=4] {'cube','row','col'}, dimensions={0} | all-to-all | bytes 2097152 | tf_op jit(solution)/shard_map/all_to_all | solution.py:49
  567.1 2.7 all-to-all-start.3
  569.8 6.1 top.1
  575.9 2.7 multiply_convert_fusion.1
  578.6 6.6 multiply_convert_fusion
  585.2 11.3 %all-to-all-done.3 = f32[32,16,512]{2,1,0:T(8,128)S(1)} async-done(((f32[32,16,512]{2,1,0:T(8,128)}), f32[32,16,512]{2,1,0:T(8,128)S(1)}, u32[]{:S(2)}, u32[]{:S(2)}) %all-to-all-start.3) | async-done | bytes 1048608 | tf_op jit(solution)/shard_map/all_to_all | solution.py:42
  596.6 28.3 %all_to_all.41 = f16[4,128,2048]{2,1,0:T(8,128)(2,1)} all-to-all(f16[4,128,2048]{2,1,0:T(8,128)(2,1)S(1)} %bitcast.117), channel_id=1, replica_groups=mesh['cube'=2,'row'=4,'col'=4] {'row'}, dimensions={0} | all-to-all | bytes 4194304 | tf_op jit(solution)/shard_map/all_to_all | solution.py:49
  624.8 4.8 all-to-all-start.4
  629.6 11.7 %cholesky.75 = f32[128,128]{1,0:T(8,128)S(1)} custom-call(f32[128,128]{1,0:T(8,128)S(1)} %slice.93), custom_call_target="Cholesky" | custom-call | tf_op jit(solution)/shard_map/jit(cholesky)/cholesky | solution.py:177
  643.3 9.8 %custom-call.8 = f32[1,128,128]{1,2,0:T(8,128)S(1)} custom-call(f32[1,128,128]{2,1,0:T(8,128)S(1)} %get-tuple-element.18), custom_call_target="InvertDiagBlocksLowerTriangular" | custom-call | tf_op jit(solution)/shard_map/jit(_solve_triangular)/triangular_solve | solution.py:178
  654.2 68.8 %all-to-all-done.4 = f16[8,512,512]{2,1,0:T(8,128)(2,1)} async-done(((f16[8,512,512]{2,1,0:T(8,128)(2,1)}), f16[8,512,512]{2,1,0:T(8,128)(2,1)}, u32[]{:S(2)}, u32[]{:S(2)}) %all-to-all-start.4) | async-done | bytes 4194336 | tf_op jit(solution)/shard_map/all_to_all | solution.py:49
  724.6 3.9 all-to-all-start.7
  729.3 11.7 %cholesky.86 = f32[128,128]{1,0:T(8,128)S(1)} custom-call(f32[128,128]{1,0:T(8,128)S(1)} %convolution_subtract_fusion.13), custom_call_target="Cholesky" | custom-call | tf_op jit(solution)/shard_map/jit(cholesky)/cholesky | solution.py:177
  743.0 9.8 %custom-call.9 = f32[1,128,128]{1,2,0:T(8,128)S(1)} custom-call(f32[1,128,128]{2,1,0:T(8,128)S(1)} %get-tuple-element.16), custom_call_target="InvertDiagBlocksLowerTriangular" | custom-call | tf_op jit(solution)/shard_map/jit(_solve_triangular)/triangular_solve | solution.py:178
  753.1 1.9 slice_bitcast_fusion.6
  755.0 3.4 broadcast_in_dim.48
  758.5 5.0 all-to-all-start.5
  770.0 13.2 %cholesky.97 = f32[128,128]{1,0:T(8,128)} custom-call(f32[128,128]{1,0:T(8,128)} %convolution_subtract_fusion.10), custom_call_target="Cholesky" | custom-call | tf_op jit(solution)/shard_map/jit(cholesky)/cholesky | solution.py:177
  784.7 2.1 select_bitcast_fusion.1
  786.8 11.3 %custom-call.10 = f32[1,128,128]{1,2,0:T(8,128)} custom-call(f32[1,128,128]{2,1,0:T(8,128)} %get-tuple-element.14), custom_call_target="InvertDiagBlocksLowerTriangular" | custom-call | tf_op jit(solution)/shard_map/jit(_solve_triangular)/triangular_solve | solution.py:178
  801.7 11.9 %cholesky.108 = f32[128,128]{1,0:T(8,128)S(1)} custom-call(f32[128,128]{1,0:T(8,128)S(1)} %convolution_subtract_fusion.4), custom_call_target="Cholesky" | custom-call | tf_op jit(solution)/shard_map/jit(cholesky)/cholesky | solution.py:177
  814.8 9.8 %custom-call.11 = f32[1,128,128]{1,2,0:T(8,128)S(1)} custom-call(f32[1,128,128]{2,1,0:T(8,128)S(1)} %get-tuple-element.12), custom_call_target="InvertDiagBlocksLowerTriangular" | custom-call | tf_op jit(solution)/shard_map/jit(_solve_triangular)/triangular_solve | solution.py:178
  831.2 2.0 fusion.18
  834.4 22.0 %all-to-all-done.5 = f16[8,512,512]{2,1,0:T(8,128)(2,1)} async-done(((f16[8,512,512]{2,1,0:T(8,128)(2,1)}), f16[8,512,512]{2,1,0:T(8,128)(2,1)}, u32[]{:S(2)}, u32[]{:S(2)}) %all-to-all-start.5) | async-done | bytes 4194336 | tf_op jit(solution)/shard_map/all_to_all | solution.py:42
  856.5 3.6 convert_multiply_fusion
  860.1 2.0 fusion.21
  864.8 4.8 convolution_subtract_fusion.1
  869.7 2.9 copy.16
  872.6 3.7 fusion.65
  877.7 9.4 convolution_subtract_fusion
  887.0 3.1 copy.17
  890.2 3.7 fusion.67
  895.2 12.5 %fusion.6 = f32[4096,128]{1,0:T(8,128)} fusion(f32[4096,128]{0,1:T(8,128)S(1)} %fusion.67, f32[4096,128]{0,1:T(8,128)S(1)} %copy-done.6, f32[4096,128]{0,1:T(8,128)S(1)} %copy-done.2, f32[4096,512]{1,0:T(8,128)} %bitcast.113, f32[128,128]{0,1:T(8,128)S(1)} %fusion.69, f32[128,128]{0,1:T(8,128)S(1)} %fusion.68, f32[128,128]{0,1:T(8,128)S(1)} %fusion.43), kind=kOutput, calls=%fused_computation.11 | convolution fusion | flops 2419687424 | bytes 10682368 | tf_op jit(solution)/shard_map/dot_general | solution.py:205
  907.8 2.9 copy.18
  910.6 3.6 fusion.70
  914.4 2.2 pad_maximum_fusion
  916.9 2.9 convert_element_type.46.rows_ref
  919.8 1.8 copy-done.3
  921.6 41.1 %final.1 = f32[4096,2048]{1,0:T(8,128)} custom-call(s32[98]{0:T(128)S(1)} %pad_add_fusion.tables, bf16[4096,2048]{1,0:T(8,128)(2,1)} %parent_ref.5, bf16[4096,512]{1,0:T(8,128)(2,1)} %convert_element_type.46.rows_ref, bf16[512,2048]{1,0:T(8,128)(2,1)S(1)} %pad_maximum_fusion.1.cols_ref, f32[2,4,4,512,256]{4,3,2,1,0:T(8,128)} %convert.17.refs_0_.refs_1_, ...), custom_call_target="tpu_custom_call" | custom-call | tf_op jit(solution)/shard_map/final/pallas_call | solution.py:151
  (129 shorter events, 40.2 us)
Async XLA Ops:
  2.4 0.8 collective-permute-start
  7.6 143.6 %copy-start.25 = (s32[2,64]{1,0:T(2,128)S(1)}, s32[2,64]{1,0:T(2,128)}, u32[]{:S(2)}) copy-start(s32[2,64]{1,0:T(2,128)} %param.10) | copy-start | bytes 1540
  7.6 238.1 %all-to-all-start = ((bf16[4,512,2048]{2,1,0:T(8,128)(2,1)}), bf16[4,512,2048]{2,1,0:T(8,128)(2,1)}, u32[]{:S(2)}, u32[]{:S(2)}) async-start(bf16[4,512,2048]{2,1,0:T(8,128)(2,1)} %broadcast_in_dim.44), calls=%async_computation | async-start | bytes 16777216 | tf_op jit(solution)/shard_map/all_to_all | solution.py:42
  308.9 186.0 %all-to-all-start.1 = ((f16[32,512,256]{2,1,0:T(8,128)(2,1)}), f16[32,512,256]{2,1,0:T(8,128)(2,1)}, u32[]{:S(2)}, u32[]{:S(2)}) async-start(f16[32,512,256]{2,1,0:T(8,128)(2,1)} %bitcast.109), calls=%async_computation.1 | async-start | bytes 16777216 | tf_op jit(solution)/shard_map/all_to_all | solution.py:265
  567.1 29.5 %all-to-all-start.3 = ((f32[32,16,512]{2,1,0:T(8,128)}), f32[32,16,512]{2,1,0:T(8,128)S(1)}, u32[]{:S(2)}, u32[]{:S(2)}) async-start(f32[32,16,512]{2,1,0:T(8,128)} %broadcast_in_dim.46), calls=%async_computation.3 | async-start | bytes 2097152 | tf_op jit(solution)/shard_map/all_to_all | solution.py:42
  624.8 98.2 %all-to-all-start.4 = ((f16[8,512,512]{2,1,0:T(8,128)(2,1)}), f16[8,512,512]{2,1,0:T(8,128)(2,1)}, u32[]{:S(2)}, u32[]{:S(2)}) async-start(f16[8,512,512]{2,1,0:T(8,128)(2,1)} %bitcast.114), calls=%async_computation.4 | async-start | bytes 8388608 | tf_op jit(solution)/shard_map/all_to_all | solution.py:49
  724.6 30.4 %all-to-all-start.7 = ((f16[4,128,2048]{2,1,0:T(8,128)(2,1)}), f16[4,128,2048]{2,1,0:T(8,128)(2,1)S(1)}, u32[]{:S(2)}, u32[]{:S(2)}) async-start(f16[4,128,2048]{2,1,0:T(8,128)(2,1)} %broadcast_in_dim.86), calls=%async_computation.7 | async-start | bytes 4194304 | tf_op jit(solution)/shard_map/all_to_all | solution.py:42
  728.8 37.8 %copy-start.10 = (f32[128,128]{1,0:T(8,128)}, f32[128,128]{1,0:T(8,128)S(1)}, u32[]{:S(2)}) copy-start(f32[128,128]{1,0:T(8,128)S(1)} %fusion.36) | copy-start | bytes 196612
  758.5 98.0 %all-to-all-start.5 = ((f16[8,512,512]{2,1,0:T(8,128)(2,1)}), f16[8,512,512]{2,1,0:T(8,128)(2,1)}, u32[]{:S(2)}, u32[]{:S(2)}) async-start(f16[8,512,512]{2,1,0:T(8,128)(2,1)} %broadcast_in_dim.48), calls=%async_computation.5 | async-start | bytes 8388608 | tf_op jit(solution)/shard_map/all_to_all | solution.py:42
  763.8 35.7 %copy-start.12 = (f32[128,128]{1,0:T(8,128)}, f32[128,128]{1,0:T(8,128)S(1)}, u32[]{:S(2)}) copy-start(f32[128,128]{1,0:T(8,128)S(1)} %fusion.34) | copy-start | bytes 196612
  799.2 0.6 copy-start.14
  824.9 0.8 copy-start.11
  825.8 2.1 copy-start.13
  827.9 2.3 copy-start.15
  860.1 3.4 copy-start.4
  863.5 1.3 copy-start
  872.6 5.1 copy-start.1
  876.3 1.4 copy-start.5
  890.1 5.1 copy-start.2
  890.1 5.1 copy-start.6
  893.9 1.4 copy-start.7
  910.6 3.6 copy-start.8
  910.6 3.6 copy-start.9
  914.3 2.3 copy-start.16
  914.3 2.3 copy-start.17
  914.3 2.3 copy-start.18
  914.3 2.3 copy-start.19
  914.3 2.3 copy-start.20
  914.3 2.3 copy-start.21
  914.3 2.3 copy-start.22
  914.3 2.3 copy-start.23
  914.4 2.3 copy-start.24
  916.9 4.7 copy-start.3
